TPU v7x, 512 devices: a whole 4x8x8 slice. The times are simulated.
512 devices in a mesh: layer: 2 (over core), row: 16 (over x, z_hi), col: 16 (over z_lo, y).
Axes of the slice: x: 4, y: 8, z: 8 (z_hi: 4, z_lo: 2; z = z_hi * 2 + z_lo), core: 2. Of those that a mesh axis runs over, the one named last changes fastest.
Arguments:
- rhs_sub: float32 [2, 3, 1, 16, 256, 512], P('layer', None, None, 'row', 'col'), may hold values from -6 to 6
- rhs_top: float32 [1, 16, 256, 512], P(None, 'row', 'col'), may hold values from -6 to 6
- lower_inv_sub: float32 [2, 3, 1, 16, 256, 256], P('layer', None, None, 'row', 'col'), as said below
- lower_inv_top: float32 [1, 16, 256, 256], P(None, 'row', 'col'), as said below
- upper_inv_sub: float32 [2, 3, 1, 16, 256, 256], P('layer', None, None, 'row', 'col'), as said below
- upper_inv_top: float32 [1, 16, 256, 256], P(None, 'row', 'col'), as said below
- lower_sub: float32 [2, 3, 1, 16, 1, 16, 256, 256], P('layer', None, None, 'row', None, 'col'), may hold values from -0.09375 to 0.09375
- lower_top: float32 [2, 3, 1, 16, 1, 16, 256, 256], P('layer', None, None, 'row', None, 'col'), may hold values from -0.0546875 to 0.0546875
- upper_sub: float32 [2, 3, 1, 16, 1, 16, 256, 256], P('layer', None, None, 'row', None, 'col'), may hold values from -0.0625 to 0.0625
- upper_top: float32 [2, 3, 1, 16, 1, 16, 256, 256], P('layer', None, None, 'row', None, 'col'), may hold values from -0.09375 to 0.09375
- block_pattern: int32 [2, 4, 3, 1, 16, 1, 16], P('layer', None, None, None, 'row', None, 'col'), may hold values 0 or 1
Outputs:
- solution_sub: float32 [2, 3, 1, 16, 256, 512], P('layer', None, None, 'row', 'col')
- solution_top: float32 [1, 16, 256, 512], P(None, 'row', 'col')
Inputs may be any that keep to these rules, and one draw needn't show every extreme that they name: `lower_inv_sub`: every 256 x 256 block is lower triangular with unit diagonal. `lower_inv_top`: every 256 x 256 block is lower triangular with unit diagonal. `upper_inv_sub`: every 256 x 256 block is upper triangular with unit diagonal. `upper_inv_top`: every 256 x 256 block is upper triangular with unit diagonal.
All inputs are finite; a program needn't handle non-finite values. No bound on the sum of `block_pattern` on one device may be relied on, other than what follows from the above.
Results may differ from a plain program's by a relative error of at most 0.00014.
Values sent between devices are 32-bit elements; how exact they have to be, the bound alone decides.
No kernel may reach another device: no remote copies, remote signals or barrier semaphores. Data moves between devices by JAX's collectives and lax.ppermute only.
A program may use at most 64 MiB of HBM per device.

v0:
```python
import jax
import jax.numpy as jnp
from jax import lax
from jax.sharding import PartitionSpec as P

HIGHEST = lax.Precision.HIGHEST


def broadcast(x, axis, root):
    mine = lax.axis_index(axis) == root
    return lax.psum(jnp.where(mine, x, jnp.zeros_like(x)), axis)


def couple(blocks, pattern, solution):
    weighted = solution[None] * pattern[:, :, None, None].astype(jnp.float32)
    return jnp.einsum("tsab,tsbn->tan", blocks, weighted, precision=HIGHEST)


def spread(whole_block):
    return broadcast(whole_block, "row", lax.axis_index("col"))


def on_device(
    rhs_sub,
    rhs_top,
    lower_inv_sub,
    lower_inv_top,
    upper_inv_sub,
    upper_inv_top,
    lower_sub,
    lower_top,
    upper_sub,
    upper_top,
    block_pattern,
):
    lower_list = [lower_inv_sub[0, level, :, 0] for level in range(3)] + [lower_inv_top[:, 0]]
    upper_list = [upper_inv_sub[0, level, :, 0] for level in range(3)] + [upper_inv_top[:, 0]]
    right_sides = [rhs_sub[0, level, :, 0] for level in range(3)] + [rhs_top[:, 0]]

    def solve(partial_value, right_side, inverse_rows, top):
        if partial_value is None:
            residual = right_side
        else:
            share = lax.psum_scatter(partial_value, "col", scatter_dimension=1, tiled=True)
            if top:
                share = lax.psum(share, "layer")
            residual = right_side - share
        return jnp.einsum(
            "kab,kbn->kan",
            inverse_rows,
            lax.all_gather(residual, "col", axis=1, tiled=True),
            precision=HIGHEST,
        )

    def copy_out(solution):
        return spread(lax.all_gather(solution, "col", axis=1, tiled=True))

    def blocks(array, pair):
        return array[0, pair, :, 0, :, 0]

    def pattern(kind, pair):
        return block_pattern[0, kind, pair, :, 0, :, 0]

    fore_zero = solve(None, right_sides[0], lower_list[0], False)
    copy_zero = copy_out(fore_zero)
    into_one = couple(blocks(lower_sub, 0), pattern(0, 0), copy_zero)
    into_two = couple(blocks(lower_sub, 1), pattern(0, 1), copy_zero)
    into_top = couple(blocks(lower_top, 0), pattern(1, 0), copy_zero)
    fore_one = solve(into_one, right_sides[1], lower_list[1], False)
    copy_one = copy_out(fore_one)
    into_two = into_two + couple(blocks(lower_sub, 2), pattern(0, 2), copy_one)
    into_top = into_top + couple(blocks(lower_top, 1), pattern(1, 1), copy_one)
    fore_two = solve(into_two, right_sides[2], lower_list[2], False)
    copy_two = copy_out(fore_two)
    into_top = into_top + couple(blocks(lower_top, 2), pattern(1, 2), copy_two)
    fore_top = solve(into_top, right_sides[3], lower_list[3], True)
    final_top = solve(None, fore_top, upper_list[3], False)
    down_top = copy_out(final_top)
    toward_two = couple(blocks(upper_top, 2), pattern(3, 2), down_top)
    toward_one = couple(blocks(upper_top, 1), pattern(3, 1), down_top)
    toward_zero = couple(blocks(upper_top, 0), pattern(3, 0), down_top)
    final_two = solve(toward_two, fore_two, upper_list[2], False)
    down_two = copy_out(final_two)
    toward_one = toward_one + couple(blocks(upper_sub, 2), pattern(2, 2), down_two)
    toward_zero = toward_zero + couple(blocks(upper_sub, 1), pattern(2, 1), down_two)
    final_one = solve(toward_one, fore_one, upper_list[1], False)
    down_one = copy_out(final_one)
    toward_zero = toward_zero + couple(blocks(upper_sub, 0), pattern(2, 0), down_one)
    final_zero = solve(toward_zero, fore_zero, upper_list[0], False)
    solution_sub = jnp.stack([final_zero, final_one, final_two])[None, :, :, None]
    solution_top = final_top[:, None]
    return (solution_sub, solution_top)


def solution(mesh):
    placed = (
        P("layer", None, None, "row", "col", None),
        P(None, "row", "col", None),
        P("layer", None, None, "row", "col", None),
        P(None, "row", "col", None),
        P("layer", None, None, "row", "col", None),
        P(None, "row", "col", None),
        P("layer", None, None, "row", None, "col", None, None),
        P("layer", None, None, "row", None, "col", None, None),
        P("layer", None, None, "row", None, "col", None, None),
        P("layer", None, None, "row", None, "col", None, None),
        P("layer", None, None, None, "row", None, "col"),
    )
    return jax.shard_map(
        on_device,
        mesh=mesh,
        in_specs=placed,
        out_specs=(P("layer", None, None, "row", "col", None), P(None, "row", "col", None)),
        check_vma=False,
    )
```

profile of v0, /device:TPU:2, one launch (start us, length us, event | category | flops | bytes accessed | tf_op | source)
XLA Modules:
  0.0 2184.0 jit_solution(2908091870607377560)
XLA Ops:
  7.2 0.8 fusion.100
  8.0 37.7 %all-gather = f32[1,1,1,1,256,512]{5,4,3,2,1,0:T(8,128)S(1)} all-gather(f32[1,1,1,1,16,512]{5,4,3,2,1,0:T(8,128)S(1)} %get-tuple-element.8), channel_id=2, replica_groups=mesh['layer'=2,'row'=16,'col'=16] {'col'}, dimensions={4}, use_global_device_ids=true | all-gather | bytes 557056 | tf_op jit(solution)/shard_map/all_gather | solution.py:51
  46.1 32.3 %all-gather.1 = f32[256,512]{1,0:T(8,128)S(1)} all-gather(f32[16,512]{1,0:T(8,128)S(1)} %fusion.33), channel_id=3, replica_groups=mesh['layer'=2,'row'=16,'col'=16] {'col'}, dimensions={0}, use_global_device_ids=true | all-gather | bytes 557056 | tf_op jit(solution)/shard_map/all_gather | solution.py:56
  78.4 0.8 select_bitcast_fusion.5
  79.3 0.6 copy-done.13
  79.9 0.7 fusion.101
  81.3 168.6 %all-reduce.13.cloned.1.call-done = f32[1,256,512]{2,1,0:T(8,128)} async-done(((f32[1,256,512]{2,1,0:T(8,128)}), f32[1,256,512]{2,1,0:T(8,128)}) %all-reduce.13.cloned.1.call-update) | async-done | bytes 524304 | tf_op jit(solution)/shard_map/psum | solution.py:11
  249.9 2.0 convolution_bitcast_fusion.1
  252.0 1.0 copy.24
  253.1 1.3 dynamic-slice
  255.0 140.9 %all-reduce.25.cloned.1.call-done = f32[1,256,512]{2,0,1:T(1,128)} async-done(((f32[1,256,512]{2,0,1:T(1,128)}), f32[1,256,512]{2,0,1:T(1,128)}) %all-reduce.25.cloned.1.call-update) | async-done | bytes 524304
  395.9 0.8 fusion.84
  396.7 35.3 %all_gather.44 = f32[1,256,512]{2,0,1:T(1,128)S(1)} all-gather(f32[1,16,512]{2,0,1:T(1,128)S(1)} %fusion.84), channel_id=1, replica_groups=mesh['layer'=2,'row'=16,'col'=16] {'col'}, dimensions={1}, use_global_device_ids=true | all-gather | bytes 557056 | tf_op jit(solution)/shard_map/all_gather | solution.py:51
  432.0 0.4 fusion.9
  432.4 32.3 %all-gather.2 = f32[256,512]{1,0:T(8,128)S(1)} all-gather(f32[16,512]{1,0:T(8,128)S(1)} %bitcast.205), channel_id=4, replica_groups=mesh['layer'=2,'row'=16,'col'=16] {'col'}, dimensions={0}, use_global_device_ids=true | all-gather | bytes 557056 | tf_op jit(solution)/shard_map/all_gather | solution.py:56
  464.7 0.9 select_bitcast_fusion.4
  467.0 1.0 fusion.27
  468.0 165.1 %all-reduce.15.cloned.1.call-done = f32[1,256,512]{2,1,0:T(8,128)} async-done(((f32[1,256,512]{2,1,0:T(8,128)}), f32[1,256,512]{2,1,0:T(8,128)}) %all-reduce.15.cloned.1.call-update) | async-done | bytes 524304 | tf_op jit(solution)/shard_map/psum | solution.py:11
  633.1 2.0 fusion.3
  635.2 1.0 copy.26
  638.1 141.0 %all-reduce.27.cloned.1.call-done = f32[1,256,512]{2,0,1:T(1,128)} async-done(((f32[1,256,512]{2,0,1:T(1,128)}), f32[1,256,512]{2,0,1:T(1,128)}) %all-reduce.27.cloned.1.call-update) | async-done | bytes 524304
  779.1 0.8 fusion.83
  779.9 35.3 %all_gather.46 = f32[1,256,512]{2,0,1:T(1,128)S(1)} all-gather(f32[1,16,512]{2,0,1:T(1,128)S(1)} %fusion.83), channel_id=1, replica_groups=mesh['layer'=2,'row'=16,'col'=16] {'col'}, dimensions={1}, use_global_device_ids=true | all-gather | bytes 557056 | tf_op jit(solution)/shard_map/all_gather | solution.py:51
  815.2 0.4 fusion.6
  815.6 32.3 %all-gather.3 = f32[256,512]{1,0:T(8,128)S(1)} all-gather(f32[16,512]{1,0:T(8,128)S(1)} %bitcast.206), channel_id=5, replica_groups=mesh['layer'=2,'row'=16,'col'=16] {'col'}, dimensions={0}, use_global_device_ids=true | all-gather | bytes 557056 | tf_op jit(solution)/shard_map/all_gather | solution.py:56
  847.9 0.9 select_bitcast_fusion.3
  849.3 1.0 fusion.31
  850.3 1.0 convolution_add_fusion.5
  851.3 165.0 %all-reduce.17.cloned.1.call-done = f32[1,256,512]{2,1,0:T(8,128)} async-done(((f32[1,256,512]{2,1,0:T(8,128)}), f32[1,256,512]{2,1,0:T(8,128)}) %all-reduce.17.cloned.1.call-update) | async-done | bytes 524304 | tf_op jit(solution)/shard_map/psum | solution.py:11
  1016.3 2.0 fusion.2
  1018.3 1.1 copy.27
  1019.5 142.8 %all-reduce.29.cloned.1.call-done = f32[1,256,512]{2,0,1:T(1,128)} async-done(((f32[1,256,512]{2,0,1:T(1,128)}), f32[1,256,512]{2,0,1:T(1,128)}) %all-reduce.29.cloned.1.call-update) | async-done | bytes 524304
  1162.3 0.8 constant_dynamic-slice_fusion
  1163.1 3.5 psum.52
  1166.7 35.3 %all_gather.48 = f32[1,256,512]{2,0,1:T(1,128)S(1)} all-gather(f32[1,16,512]{2,0,1:T(1,128)S(1)} %reshape_subtract_fusion), channel_id=1, replica_groups=mesh['layer'=2,'row'=16,'col'=16] {'col'}, dimensions={1}, use_global_device_ids=true | all-gather | bytes 557056 | tf_op jit(solution)/shard_map/all_gather | solution.py:51
  1201.9 0.4 convolution_bitcast_fusion.3
  1202.3 32.8 %all-gather.4 = f32[256,512]{1,0:T(8,128)S(1)} all-gather(f32[16,512]{1,0:T(8,128)S(1)} %convolution_bitcast_fusion.3), channel_id=6, replica_groups=mesh['layer'=2,'row'=16,'col'=16] {'col'}, dimensions={0}, use_global_device_ids=true | all-gather | bytes 557056 | tf_op jit(solution)/shard_map/all_gather | solution.py:51
  1235.1 0.4 fusion.88
  1235.5 34.6 %all-gather.5 = f32[256,512]{1,0:T(8,128)S(1)} all-gather(f32[16,512]{1,0:T(8,128)S(1)} %bitcast.211), channel_id=7, replica_groups=mesh['layer'=2,'row'=16,'col'=16] {'col'}, dimensions={0}, use_global_device_ids=true | all-gather | bytes 557056 | tf_op jit(solution)/shard_map/all_gather | solution.py:56
  1270.0 0.8 select_bitcast_fusion.2
  1271.6 165.4 %all-reduce.19.cloned.1.call-done = f32[1,256,512]{2,1,0:T(8,128)} async-done(((f32[1,256,512]{2,1,0:T(8,128)}), f32[1,256,512]{2,1,0:T(8,128)}) %all-reduce.19.cloned.1.call-update) | async-done | bytes 524304 | tf_op jit(solution)/shard_map/psum | solution.py:11
  1437.0 2.5 convolution_bitcast_fusion
  1439.5 75.0 %reduce-scatter.4.cloned.1.call-done = f32[1,16,512]{2,1,0:T(8,128)} async-done(((f32[1,256,512]{2,1,0:T(8,128)}), f32[1,16,512]{2,1,0:T(8,128)}) %reduce-scatter.4.cloned.1.call-update) | async-done | bytes 32784 | tf_op jit(solution)/shard_map/reduce_scatter | solution.py:44
  1514.6 0.8 bitcast_subtract_fusion.1
  1515.3 33.9 %all_gather.51 = f32[1,256,512]{2,1,0:T(8,128)S(1)} all-gather(f32[1,16,512]{2,1,0:T(8,128)S(1)} %bitcast_subtract_fusion.1), channel_id=1, replica_groups=mesh['layer'=2,'row'=16,'col'=16] {'col'}, dimensions={1}, use_global_device_ids=true | all-gather | bytes 557056 | tf_op jit(solution)/shard_map/all_gather | solution.py:51
  1549.2 0.4 fusion.20
  1549.6 33.3 %all-gather.6 = f32[256,512]{1,0:T(8,128)S(1)} all-gather(f32[16,512]{1,0:T(8,128)S(1)} %bitcast.207), channel_id=8, replica_groups=mesh['layer'=2,'row'=16,'col'=16] {'col'}, dimensions={0}, use_global_device_ids=true | all-gather | bytes 557056 | tf_op jit(solution)/shard_map/all_gather | solution.py:56
  1582.9 0.9 select_bitcast_fusion.1
  1585.6 0.7 fusion.17
  1586.2 164.1 %all-reduce.21.cloned.1.call-done = f32[1,256,512]{2,1,0:T(8,128)} async-done(((f32[1,256,512]{2,1,0:T(8,128)}), f32[1,256,512]{2,1,0:T(8,128)}) %all-reduce.21.cloned.1.call-update) | async-done | bytes 524304 | tf_op jit(solution)/shard_map/psum | solution.py:11
  1750.4 2.5 fusion.1
  1754.8 73.1 %reduce-scatter.6.cloned.1.call-done = f32[1,16,512]{2,1,0:T(8,128)} async-done(((f32[1,256,512]{2,1,0:T(8,128)}), f32[1,16,512]{2,1,0:T(8,128)}) %reduce-scatter.6.cloned.1.call-update) | async-done | bytes 32784 | tf_op jit(solution)/shard_map/reduce_scatter | solution.py:44
  1827.9 0.8 bitcast_subtract_fusion
  1828.6 33.8 %all_gather.53 = f32[1,256,512]{2,1,0:T(8,128)S(1)} all-gather(f32[1,16,512]{2,1,0:T(8,128)S(1)} %bitcast_subtract_fusion), channel_id=1, replica_groups=mesh['layer'=2,'row'=16,'col'=16] {'col'}, dimensions={1}, use_global_device_ids=true | all-gather | bytes 557056 | tf_op jit(solution)/shard_map/all_gather | solution.py:51
  1862.8 33.3 %all-gather.7 = f32[256,512]{1,0:T(8,128)S(1)} all-gather(f32[16,512]{1,0:T(8,128)S(1)} %bitcast.209), channel_id=9, replica_groups=mesh['layer'=2,'row'=16,'col'=16] {'col'}, dimensions={0}, use_global_device_ids=true | all-gather | bytes 557056 | tf_op jit(solution)/shard_map/all_gather | solution.py:56
  1896.1 0.9 select_bitcast_fusion
  1897.1 0.7 fusion.23
  1898.1 0.7 convolution_add_fusion.2
  1898.8 165.3 %all-reduce.23.cloned.1.call-done = f32[1,256,512]{2,1,0:T(8,128)} async-done(((f32[1,256,512]{2,1,0:T(8,128)}), f32[1,256,512]{2,1,0:T(8,128)}) %all-reduce.23.cloned.1.call-update) | async-done | bytes 524304 | tf_op jit(solution)/shard_map/psum | solution.py:11
  2064.1 2.5 fusion
  2066.6 75.0 %reduce-scatter.8.cloned.1.call-done = f32[1,16,512]{2,1,0:T(8,128)} async-done(((f32[1,256,512]{2,1,0:T(8,128)}), f32[1,16,512]{2,1,0:T(8,128)}) %reduce-scatter.8.cloned.1.call-update) | async-done | bytes 32784 | tf_op jit(solution)/shard_map/reduce_scatter | solution.py:44
  2141.6 0.8 bitcast_subtract_fusion.2
  2142.4 33.8 %all_gather.55 = f32[1,256,512]{2,1,0:T(8,128)S(1)} all-gather(f32[1,16,512]{2,1,0:T(8,128)S(1)} %bitcast_subtract_fusion.2), channel_id=1, replica_groups=mesh['layer'=2,'row'=16,'col'=16] {'col'}, dimensions={1}, use_global_device_ids=true | all-gather | bytes 557056 | tf_op jit(solution)/shard_map/all_gather | solution.py:51
  2176.5 0.7 maximum_bitcast_fusion
  (57 shorter events, 2.9 us)
Async XLA Ops:
  7.2 1194.8 %copy-start = (f32[1,1,16,256]{3,2,1,0:T(8,128)S(1)}, f32[1,1,16,256]{3,2,1,0:T(8,128)}, u32[]{:S(2)}) copy-start(f32[1,1,16,256]{3,2,1,0:T(8,128)} %param.14) | copy-start | bytes 49156
  7.2 242.7 %all-reduce.13.cloned.1.call-start = ((), (), s32[]{:S(2)}) async-start(), calls=%async_computation.3 | async-start | bytes 1048576 | tf_op jit(solution)/shard_map/psum | solution.py:11
  8.0 37.7 %copy-start.10 = (f32[1,3,1,1,16,256]{5,4,3,2,1,0:T(8,128)S(1)}, f32[1,3,1,1,16,256]{5,4,3,2,1,0:T(8,128)}, u32[]{:S(2)}) copy-start(f32[1,3,1,1,16,256]{5,4,3,2,1,0:T(8,128)} %param.13) | copy-start | bytes 147460
  78.4 171.5 %copy-start.6 = (f32[1,3,1,1,1,1,256,256]{7,6,5,4,3,2,1,0:T(8,128)S(1)}, f32[1,3,1,1,1,1,256,256]{7,6,5,4,3,2,1,0:T(8,128)}, u32[]{:S(2)}) copy-start(f32[1,3,1,1,1,1,256,256]{7,6,5,4,3,2,1,0:T(8,128)} %param.17) | copy-start | bytes 2359300
  79.3 0.7 copy-start.13
  79.3 316.6 %all-reduce.25.cloned.1.call-start = ((), (), s32[]{:S(2)}) async-start(), calls=%async_computation.12 | async-start | bytes 1048576
  253.0 380.1 %all-reduce.15.cloned.1.call-start = ((), (), s32[]{:S(2)}) async-start(), calls=%async_computation.4 | async-start | bytes 1048576 | tf_op jit(solution)/shard_map/psum | solution.py:11
  465.6 1.4 copy-start.1
  465.6 313.5 %all-reduce.27.cloned.1.call-start = ((), (), s32[]{:S(2)}) async-start(), calls=%async_computation.13 | async-start | bytes 1048576
  636.2 380.1 %all-reduce.17.cloned.1.call-start = ((), (), s32[]{:S(2)}) async-start(), calls=%async_computation.5 | async-start | bytes 1048576 | tf_op jit(solution)/shard_map/psum | solution.py:11
  847.9 1.3 copy-start.7
  848.8 313.5 %all-reduce.29.cloned.1.call-start = ((), (), s32[]{:S(2)}) async-start(), calls=%async_computation.14 | async-start | bytes 1048576
  849.3 1.0 copy-start.3
  1019.4 417.5 %all-reduce.19.cloned.1.call-start = ((), (), s32[]{:S(2)}) async-start(), calls=%async_computation.6 | async-start | bytes 1048576 | tf_op jit(solution)/shard_map/psum | solution.py:11
  1163.1 3.5 copy-start.12
  1202.3 32.8 %copy-start.14 = (f32[1,1,16,256]{3,2,1,0:T(8,128)S(1)}, f32[1,1,16,256]{3,2,1,0:T(8,128)}, u32[]{:S(2)}) copy-start(f32[1,1,16,256]{3,2,1,0:T(8,128)} %param.16) | copy-start | bytes 49156
  1235.5 34.6 %copy-start.9 = (f32[512,16]{0,1:T(8,128)}, f32[512,16]{0,1:T(8,128)S(1)}, u32[]{:S(2)}) copy-start(f32[512,16]{0,1:T(8,128)S(1)} %fusion.88) | copy-start | bytes 98308
  1270.0 166.9 %copy-start.5 = (f32[1,3,1,1,1,1,256,256]{7,6,5,4,3,2,1,0:T(8,128)S(1)}, f32[1,3,1,1,1,1,256,256]{7,6,5,4,3,2,1,0:T(8,128)}, u32[]{:S(2)}) copy-start(f32[1,3,1,1,1,1,256,256]{7,6,5,4,3,2,1,0:T(8,128)} %param.20) | copy-start | bytes 2359300
  1270.9 243.7 %reduce-scatter.4.cloned.1.call-start = ((), (), s32[]{:S(2)}) async-start(), calls=%async_computation.7 | async-start | bytes 557056 | tf_op jit(solution)/shard_map/reduce_scatter | solution.py:44
  1439.5 310.9 %all-reduce.21.cloned.1.call-start = ((), (), s32[]{:S(2)}) async-start(), calls=%async_computation.8 | async-start | bytes 1048576 | tf_op jit(solution)/shard_map/psum | solution.py:11
  1515.3 33.9 %copy-start.11 = (f32[1,3,1,1,16,256]{5,4,3,2,1,0:T(8,128)S(1)}, f32[1,3,1,1,16,256]{5,4,3,2,1,0:T(8,128)}, u32[]{:S(2)}) copy-start(f32[1,3,1,1,16,256]{5,4,3,2,1,0:T(8,128)} %param.15) | copy-start | bytes 147460
  1583.8 1.8 copy-start.2
  1583.8 166.6 %copy-start.8 = (f32[1,3,1,1,1,1,256,256]{7,6,5,4,3,2,1,0:T(8,128)S(1)}, f32[1,3,1,1,1,1,256,256]{7,6,5,4,3,2,1,0:T(8,128)}, u32[]{:S(2)}) copy-start(f32[1,3,1,1,1,1,256,256]{7,6,5,4,3,2,1,0:T(8,128)} %param.19) | copy-start | bytes 2359300
  1583.8 244.0 %reduce-scatter.6.cloned.1.call-start = ((), (), s32[]{:S(2)}) async-start(), calls=%async_computation.9 | async-start | bytes 557056 | tf_op jit(solution)/shard_map/reduce_scatter | solution.py:44
  1752.9 311.2 %all-reduce.23.cloned.1.call-start = ((), (), s32[]{:S(2)}) async-start(), calls=%async_computation.10 | async-start | bytes 1048576 | tf_op jit(solution)/shard_map/psum | solution.py:11
  1897.0 244.6 %reduce-scatter.8.cloned.1.call-start = ((), (), s32[]{:S(2)}) async-start(), calls=%async_computation.11 | async-start | bytes 557056 | tf_op jit(solution)/shard_map/reduce_scatter | solution.py:44
  1897.1 1.0 copy-start.4
Sparse Core Ops, SparseCore 0:
  79.4 170.4 all-reduce.12
  253.1 142.7 all-reduce.24
  465.8 167.2 all-reduce.14
  636.3 142.7 all-reduce.26
  849.0 167.2 all-reduce.16
  1019.6 142.7 all-reduce.28
  1271.0 165.8 all-reduce.18
  1439.7 74.7 reduce-scatter.3
  1583.9 166.4 all-reduce.20
  1753.0 74.7 reduce-scatter.5
  1897.1 166.9 all-reduce.22
  2066.8 74.7 reduce-scatter.7
where the time goes:
time: 2190 us; the launch traced here: 2180 us
  waiting for transfers between devices  1640 us (75%)
  blocking collectives  479 us (22%)
  between operations  22.8 us (1%)
    psum x6, waiting for transfers between devices, broadcast(): return lax.psum(jnp.where(mine, x, jnp.zeros_like(x)), axis)  994 us
    unnamed x15, waiting for transfers between devices  425 us
    all_gather x8, blocking collectives, solve(): lax.all_gather(residual, 'col', axis=1, tiled=True)  278 us
    reduce_scatter x3, waiting for transfers between devices, solve(): lax.psum_scatter(partial_value, 'col', scatter_dimension=1, tiled=True)  223 us
    all_gather x6, blocking collectives, copy_out(): return spread(lax.all_gather(solution, 'col', axis=1, tiled=True))  198 us
  transfers between devices with their start and end apart: 12, of which 12 were waited for; matrix products, arithmetic and copies ran while one was open for 0% of the time, Pallas kernels for 0%

commit v1 on v0

--- a/solution.py
+++ b/solution.py
@@ -2,13 +2,14 @@
 import jax.numpy as jnp
 from jax import lax
 from jax.sharding import PartitionSpec as P
+from jax.lax import all_gather
 
 HIGHEST = lax.Precision.HIGHEST
 
 
 def broadcast(x, axis, root):
     mine = lax.axis_index(axis) == root
-    return lax.psum(jnp.where(mine, x, jnp.zeros_like(x)), axis)
+    return jnp.sum(all_gather(jnp.where(mine, x, jnp.zeros_like(x)), axis_name=axis), 0)
 
 
 def couple(blocks, pattern, solution):

time: 2190 us -> 1900 us (0.87)
  waiting for transfers between devices: 1640 us -> 1340 us
  other arithmetic: 9.74 us -> 36.2 us
    psum x6 -> x0, waiting for transfers between devices: 994 us -> none  [broadcast(): return lax.psum(jnp.where(mine, x, jnp.zeros_like(x)), axis)]
    all_gather x0 -> x6, waiting for transfers between devices: none -> 707 us  [broadcast(): all_gather(jnp.where(mine, x, jnp.zeros_like(x)), axis_name=axis)]
    reduce_sum x0 -> x6, other arithmetic: none -> 26.4 us  [broadcast(): jnp.sum(all_gather(jnp.where(mine, x, jnp.zeros_like(x)), axis_name=axis)...]
  transfers between devices with their start and end apart: 12 -> 12, of which waited for: 12 -> 12; matrix products, arithmetic and copies ran while one was open for 0% -> 1% of each run, Pallas kernels for 0% -> 0%
where the time goes in v1:
time: 1900 us
  waiting for transfers between devices  1340 us (71%)
  blocking collectives  479 us (25%)
  other arithmetic  36.2 us (2%)
  between operations  22.4 us (1%)
  matrix products  19.2 us (1%)
    all_gather x6, waiting for transfers between devices, broadcast(): all_gather(jnp.where(mine, x, jnp.zeros_like(x)), axis_name=axis)  707 us
    unnamed x15, waiting for transfers between devices  416 us
    all_gather x8, blocking collectives, solve(): lax.all_gather(residual, 'col', axis=1, tiled=True)  278 us
    reduce_scatter x3, waiting for transfers between devices, solve(): lax.psum_scatter(partial_value, 'col', scatter_dimension=1, tiled=True)  214 us
    all_gather x6, blocking collectives, copy_out(): return spread(lax.all_gather(solution, 'col', axis=1, tiled=True))  197 us
  transfers between devices with their start and end apart: 12, of which 12 were waited for; matrix products, arithmetic and copies ran while one was open for 1% of the time, Pallas kernels for 0%

profile of v1, /device:TPU:2, one launch (start us, length us, event | category | flops | bytes accessed | tf_op | source)
XLA Modules:
  0.0 1903.0 jit_solution(3905579566187182447)
XLA Ops:
  7.3 0.9 fusion.88
  8.1 37.8 %all-gather = f32[1,1,1,1,256,512]{5,4,3,2,1,0:T(8,128)S(1)} all-gather(f32[1,1,1,1,16,512]{5,4,3,2,1,0:T(8,128)S(1)} %get-tuple-element.8), channel_id=2, replica_groups=mesh['layer'=2,'row'=16,'col'=16] {'col'}, dimensions={4}, use_global_device_ids=true | all-gather | bytes 557056 | tf_op jit(solution)/shard_map/all_gather | solution.py:52
  45.9 1.1 fusion.17
  47.0 32.3 %all-gather.1 = f32[256,512]{1,0:T(8,128)S(1)} all-gather(f32[16,512]{1,0:T(8,128)S(1)} %fusion.17), channel_id=3, replica_groups=mesh['layer'=2,'row'=16,'col'=16] {'col'}, dimensions={0}, use_global_device_ids=true | all-gather | bytes 557056 | tf_op jit(solution)/shard_map/all_gather | solution.py:57
  79.3 0.9 broadcast_select_fusion.5
  80.2 1.5 fusion.89
  82.5 121.2 %all-gather.27.cloned.1.call-done = f32[4096,512]{1,0:T(8,128)} async-done(((f32[256,512]{1,0:T(8,128)}), f32[4096,512]{1,0:T(8,128)}) %all-gather.27.cloned.1.call-update) | async-done | bytes 8388624 | tf_op jit(solution)/shard_map/all_gather | solution.py:12
  203.7 4.4 reduce.6
  208.1 1.0 convolution_bitcast_fusion.1
  209.1 1.0 copy.24
  210.3 1.3 dynamic-slice
  212.2 137.4 %all-reduce.7.cloned.1.call-done = f32[1,256,512]{2,0,1:T(1,128)} async-done(((f32[1,256,512]{2,0,1:T(1,128)}), f32[1,256,512]{2,0,1:T(1,128)}) %all-reduce.7.cloned.1.call-update) | async-done | bytes 524304
  349.5 0.8 fusion.72
  350.4 35.3 %all_gather.82 = f32[1,256,512]{2,0,1:T(1,128)S(1)} all-gather(f32[1,16,512]{2,0,1:T(1,128)S(1)} %fusion.72), channel_id=1, replica_groups=mesh['layer'=2,'row'=16,'col'=16] {'col'}, dimensions={1}, use_global_device_ids=true | all-gather | bytes 557056 | tf_op jit(solution)/shard_map/all_gather | solution.py:52
  386.1 32.3 %all-gather.3 = f32[256,512]{1,0:T(8,128)S(1)} all-gather(f32[16,512]{1,0:T(8,128)S(1)} %bitcast.169), channel_id=5, replica_groups=mesh['layer'=2,'row'=16,'col'=16] {'col'}, dimensions={0}, use_global_device_ids=true | all-gather | bytes 557056 | tf_op jit(solution)/shard_map/all_gather | solution.py:57
  418.4 0.9 broadcast_select_fusion.4
  420.5 1.0 fusion.29
  421.5 118.3 %all-gather.29.cloned.1.call-done = f32[4096,512]{1,0:T(8,128)} async-done(((f32[256,512]{1,0:T(8,128)}), f32[4096,512]{1,0:T(8,128)}) %all-gather.29.cloned.1.call-update) | async-done | bytes 8388624 | tf_op jit(solution)/shard_map/all_gather | solution.py:12
  539.8 4.4 reduce.7
  544.2 1.0 fusion.3
  545.3 1.0 copy.26
  546.4 139.3 %all-reduce.9.cloned.1.call-done = f32[1,256,512]{2,0,1:T(1,128)} async-done(((f32[1,256,512]{2,0,1:T(1,128)}), f32[1,256,512]{2,0,1:T(1,128)}) %all-reduce.9.cloned.1.call-update) | async-done | bytes 524304
  685.7 0.8 fusion.71
  686.5 35.3 %all_gather.86 = f32[1,256,512]{2,0,1:T(1,128)S(1)} all-gather(f32[1,16,512]{2,0,1:T(1,128)S(1)} %fusion.71), channel_id=1, replica_groups=mesh['layer'=2,'row'=16,'col'=16] {'col'}, dimensions={1}, use_global_device_ids=true | all-gather | bytes 557056 | tf_op jit(solution)/shard_map/all_gather | solution.py:52
  722.2 32.3 %all-gather.5 = f32[256,512]{1,0:T(8,128)S(1)} all-gather(f32[16,512]{1,0:T(8,128)S(1)} %bitcast.170), channel_id=7, replica_groups=mesh['layer'=2,'row'=16,'col'=16] {'col'}, dimensions={0}, use_global_device_ids=true | all-gather | bytes 557056 | tf_op jit(solution)/shard_map/all_gather | solution.py:57
  754.5 0.9 broadcast_select_fusion.3
  757.5 2.0 fusion.33
  759.4 2.0 convolution_add_fusion.5
  761.4 114.6 %all-gather.31.cloned.1.call-done = f32[4096,512]{1,0:T(8,128)} async-done(((f32[256,512]{1,0:T(8,128)}), f32[4096,512]{1,0:T(8,128)}) %all-gather.31.cloned.1.call-update) | async-done | bytes 8388624 | tf_op jit(solution)/shard_map/all_gather | solution.py:12
  876.0 4.4 reduce.8
  880.4 2.0 fusion.2
  882.4 1.0 copy.27
  883.6 139.3 %all-reduce.11.cloned.1.call-done = f32[1,256,512]{2,0,1:T(1,128)} async-done(((f32[1,256,512]{2,0,1:T(1,128)}), f32[1,256,512]{2,0,1:T(1,128)}) %all-reduce.11.cloned.1.call-update) | async-done | bytes 524304
  1022.9 0.8 constant_dynamic-slice_fusion
  1023.6 3.4 psum.7
  1027.1 35.3 %all_gather.90 = f32[1,256,512]{2,0,1:T(1,128)S(1)} all-gather(f32[1,16,512]{2,0,1:T(1,128)S(1)} %reshape_subtract_fusion), channel_id=1, replica_groups=mesh['layer'=2,'row'=16,'col'=16] {'col'}, dimensions={1}, use_global_device_ids=true | all-gather | bytes 557056 | tf_op jit(solution)/shard_map/all_gather | solution.py:52
  1062.8 32.6 %all-gather.7 = f32[256,512]{1,0:T(8,128)S(1)} all-gather(f32[16,512]{1,0:T(8,128)S(1)} %convolution_bitcast_fusion.3), channel_id=9, replica_groups=mesh['layer'=2,'row'=16,'col'=16] {'col'}, dimensions={0}, use_global_device_ids=true | all-gather | bytes 557056 | tf_op jit(solution)/shard_map/all_gather | solution.py:52
  1095.8 34.6 %all-gather.8 = f32[256,512]{1,0:T(8,128)S(1)} all-gather(f32[16,512]{1,0:T(8,128)S(1)} %bitcast.175), channel_id=10, replica_groups=mesh['layer'=2,'row'=16,'col'=16] {'col'}, dimensions={0}, use_global_device_ids=true | all-gather | bytes 557056 | tf_op jit(solution)/shard_map/all_gather | solution.py:57
  1130.4 0.9 broadcast_select_fusion.2
  1131.9 118.5 %all-gather.33.cloned.1.call-done = f32[4096,512]{1,0:T(8,128)} async-done(((f32[256,512]{1,0:T(8,128)}), f32[4096,512]{1,0:T(8,128)}) %all-gather.33.cloned.1.call-update) | async-done | bytes 8388624 | tf_op jit(solution)/shard_map/all_gather | solution.py:12
  1250.4 4.4 reduce.9
  1254.8 1.5 convolution_bitcast_fusion
  1256.3 71.4 %reduce-scatter.4.cloned.1.call-done = f32[1,16,512]{2,1,0:T(8,128)} async-done(((f32[1,256,512]{2,1,0:T(8,128)}), f32[1,16,512]{2,1,0:T(8,128)}) %reduce-scatter.4.cloned.1.call-update) | async-done | bytes 32784 | tf_op jit(solution)/shard_map/reduce_scatter | solution.py:45
  1327.7 0.8 bitcast_subtract_fusion.1
  1328.5 33.8 %all_gather.95 = f32[1,256,512]{2,1,0:T(8,128)S(1)} all-gather(f32[1,16,512]{2,1,0:T(8,128)S(1)} %bitcast_subtract_fusion.1), channel_id=1, replica_groups=mesh['layer'=2,'row'=16,'col'=16] {'col'}, dimensions={1}, use_global_device_ids=true | all-gather | bytes 557056 | tf_op jit(solution)/shard_map/all_gather | solution.py:52
  1362.7 33.3 %all-gather.10 = f32[256,512]{1,0:T(8,128)S(1)} all-gather(f32[16,512]{1,0:T(8,128)S(1)} %bitcast.171), channel_id=12, replica_groups=mesh['layer'=2,'row'=16,'col'=16] {'col'}, dimensions={0}, use_global_device_ids=true | all-gather | bytes 557056 | tf_op jit(solution)/shard_map/all_gather | solution.py:57
  1396.0 0.9 broadcast_select_fusion.1
  1398.3 0.7 fusion.21
  1398.9 117.9 %all-gather.35.cloned.1.call-done = f32[4096,512]{1,0:T(8,128)} async-done(((f32[256,512]{1,0:T(8,128)}), f32[4096,512]{1,0:T(8,128)}) %all-gather.35.cloned.1.call-update) | async-done | bytes 8388624 | tf_op jit(solution)/shard_map/all_gather | solution.py:12
  1516.8 4.4 reduce.10
  1521.2 1.5 fusion.1
  1522.8 71.4 %reduce-scatter.6.cloned.1.call-done = f32[1,16,512]{2,1,0:T(8,128)} async-done(((f32[1,256,512]{2,1,0:T(8,128)}), f32[1,16,512]{2,1,0:T(8,128)}) %reduce-scatter.6.cloned.1.call-update) | async-done | bytes 32784 | tf_op jit(solution)/shard_map/reduce_scatter | solution.py:45
  1594.2 0.8 bitcast_subtract_fusion
  1595.0 34.3 %all_gather.99 = f32[1,256,512]{2,1,0:T(8,128)S(1)} all-gather(f32[1,16,512]{2,1,0:T(8,128)S(1)} %bitcast_subtract_fusion), channel_id=1, replica_groups=mesh['layer'=2,'row'=16,'col'=16] {'col'}, dimensions={1}, use_global_device_ids=true | all-gather | bytes 557056 | tf_op jit(solution)/shard_map/all_gather | solution.py:52
  1629.7 32.6 %all-gather.12 = f32[256,512]{1,0:T(8,128)S(1)} all-gather(f32[16,512]{1,0:T(8,128)S(1)} %bitcast.173), channel_id=14, replica_groups=mesh['layer'=2,'row'=16,'col'=16] {'col'}, dimensions={0}, use_global_device_ids=true | all-gather | bytes 557056 | tf_op jit(solution)/shard_map/all_gather | solution.py:57
  1662.2 0.9 broadcast_select_fusion
  1665.2 0.7 fusion.25
  1665.8 0.7 convolution_add_fusion.2
  1666.5 116.5 %all-gather.37.cloned.1.call-done = f32[4096,512]{1,0:T(8,128)} async-done(((f32[256,512]{1,0:T(8,128)}), f32[4096,512]{1,0:T(8,128)}) %all-gather.37.cloned.1.call-update) | async-done | bytes 8388624 | tf_op jit(solution)/shard_map/all_gather | solution.py:12
  1783.0 4.4 reduce.11
  1787.4 1.5 fusion
  1788.9 71.5 %reduce-scatter.8.cloned.1.call-done = f32[1,16,512]{2,1,0:T(8,128)} async-done(((f32[1,256,512]{2,1,0:T(8,128)}), f32[1,16,512]{2,1,0:T(8,128)}) %reduce-scatter.8.cloned.1.call-update) | async-done | bytes 32784 | tf_op jit(solution)/shard_map/reduce_scatter | solution.py:45
  1860.4 0.8 bitcast_subtract_fusion.2
  1861.1 34.0 %all_gather.103 = f32[1,256,512]{2,1,0:T(8,128)S(1)} all-gather(f32[1,16,512]{2,1,0:T(8,128)S(1)} %bitcast_subtract_fusion.2), channel_id=1, replica_groups=mesh['layer'=2,'row'=16,'col'=16] {'col'}, dimensions={1}, use_global_device_ids=true | all-gather | bytes 557056 | tf_op jit(solution)/shard_map/all_gather | solution.py:52
  (51 shorter events, 4.6 us)
Async XLA Ops:
  7.2 1055.2 %copy-start = (f32[1,1,16,256]{3,2,1,0:T(8,128)S(1)}, f32[1,1,16,256]{3,2,1,0:T(8,128)}, u32[]{:S(2)}) copy-start(f32[1,1,16,256]{3,2,1,0:T(8,128)} %param.14) | copy-start | bytes 49156
  7.2 378.5 %copy-start.5 = (f32[1,3,1,1,16,256]{5,4,3,2,1,0:T(8,128)S(1)}, f32[1,3,1,1,16,256]{5,4,3,2,1,0:T(8,128)}, u32[]{:S(2)}) copy-start(f32[1,3,1,1,16,256]{5,4,3,2,1,0:T(8,128)} %param.13) | copy-start | bytes 147460
  7.2 200.9 %copy-start.2 = (f32[1,3,1,1,1,1,256,256]{7,6,5,4,3,2,1,0:T(8,128)S(1)}, f32[1,3,1,1,1,1,256,256]{7,6,5,4,3,2,1,0:T(8,128)}, u32[]{:S(2)}) copy-start(f32[1,3,1,1,1,1,256,256]{7,6,5,4,3,2,1,0:T(8,128)} %param.17) | copy-start | bytes 2359300
  7.2 196.5 %all-gather.27.cloned.1.call-start = ((), (), s32[]{:S(2)}) async-start(), calls=%async_computation.6 | async-start | bytes 8912896 | tf_op jit(solution)/shard_map/all_gather | solution.py:12
  80.2 269.3 %all-reduce.7.cloned.1.call-start = ((), (), s32[]{:S(2)}) async-start(), calls=%async_computation.12 | async-start | bytes 1048576
  210.2 329.6 %all-gather.29.cloned.1.call-start = ((), (), s32[]{:S(2)}) async-start(), calls=%async_computation.7 | async-start | bytes 8912896 | tf_op jit(solution)/shard_map/all_gather | solution.py:12
  419.3 266.4 %all-reduce.9.cloned.1.call-start = ((), (), s32[]{:S(2)}) async-start(), calls=%async_computation.13 | async-start | bytes 1048576
  546.3 329.7 %all-gather.31.cloned.1.call-start = ((), (), s32[]{:S(2)}) async-start(), calls=%async_computation.8 | async-start | bytes 8912896 | tf_op jit(solution)/shard_map/all_gather | solution.py:12
  754.5 272.5 %copy-start.7 = (f32[1,1,16,512]{3,2,1,0:T(8,128)S(1)}, f32[1,1,16,512]{3,2,1,0:T(8,128)}, u32[]{:S(2)}) copy-start(f32[1,1,16,512]{3,2,1,0:T(8,128)} %param.12) | copy-start | bytes 98308
  755.4 267.5 %all-reduce.11.cloned.1.call-start = ((), (), s32[]{:S(2)}) async-start(), calls=%async_computation.14 | async-start | bytes 1048576
  757.5 337.9 %copy-start.8 = (f32[1,1,16,256]{3,2,1,0:T(8,128)S(1)}, f32[1,1,16,256]{3,2,1,0:T(8,128)}, u32[]{:S(2)}) copy-start(f32[1,1,16,256]{3,2,1,0:T(8,128)} %param.16) | copy-start | bytes 49156
  880.4 374.4 %copy-start.1 = (f32[1,3,1,1,1,1,256,256]{7,6,5,4,3,2,1,0:T(8,128)S(1)}, f32[1,3,1,1,1,1,256,256]{7,6,5,4,3,2,1,0:T(8,128)}, u32[]{:S(2)}) copy-start(f32[1,3,1,1,1,1,256,256]{7,6,5,4,3,2,1,0:T(8,128)} %param.20) | copy-start | bytes 2359300
  883.5 478.8 %copy-start.6 = (f32[1,3,1,1,16,256]{5,4,3,2,1,0:T(8,128)S(1)}, f32[1,3,1,1,16,256]{5,4,3,2,1,0:T(8,128)}, u32[]{:S(2)}) copy-start(f32[1,3,1,1,16,256]{5,4,3,2,1,0:T(8,128)} %param.15) | copy-start | bytes 147460
  883.5 366.9 %all-gather.33.cloned.1.call-start = ((), (), s32[]{:S(2)}) async-start(), calls=%async_computation.9 | async-start | bytes 8912896 | tf_op jit(solution)/shard_map/all_gather | solution.py:12
  1095.8 303.1 %copy-start.4 = (f32[512,16]{0,1:T(8,128)}, f32[512,16]{0,1:T(8,128)S(1)}, u32[]{:S(2)}) copy-start(f32[512,16]{0,1:T(8,128)S(1)} %fusion.76) | copy-start | bytes 98308
  1131.3 196.5 %reduce-scatter.4.cloned.1.call-start = ((), (), s32[]{:S(2)}) async-start(), calls=%async_computation.3 | async-start | bytes 557056 | tf_op jit(solution)/shard_map/reduce_scatter | solution.py:45
  1254.8 266.4 %copy-start.3 = (f32[1,3,1,1,1,1,256,256]{7,6,5,4,3,2,1,0:T(8,128)S(1)}, f32[1,3,1,1,1,1,256,256]{7,6,5,4,3,2,1,0:T(8,128)}, u32[]{:S(2)}) copy-start(f32[1,3,1,1,1,1,256,256]{7,6,5,4,3,2,1,0:T(8,128)} %param.19) | copy-start | bytes 2359300
  1256.3 260.5 %all-gather.35.cloned.1.call-start = ((), (), s32[]{:S(2)}) async-start(), calls=%async_computation.10 | async-start | bytes 8912896 | tf_op jit(solution)/shard_map/all_gather | solution.py:12
  1396.9 197.3 %reduce-scatter.6.cloned.1.call-start = ((), (), s32[]{:S(2)}) async-start(), calls=%async_computation.4 | async-start | bytes 557056 | tf_op jit(solution)/shard_map/reduce_scatter | solution.py:45
  1522.7 260.3 %all-gather.37.cloned.1.call-start = ((), (), s32[]{:S(2)}) async-start(), calls=%async_computation.11 | async-start | bytes 8912896 | tf_op jit(solution)/shard_map/all_gather | solution.py:12
  1663.1 197.2 %reduce-scatter.8.cloned.1.call-start = ((), (), s32[]{:S(2)}) async-start(), calls=%async_computation.5 | async-start | bytes 557056 | tf_op jit(solution)/shard_map/reduce_scatter | solution.py:45
Sparse Core Ops, SparseCore 0:
  80.3 123.3 all-gather.26
  210.3 139.1 all-reduce.6
  419.4 120.4 all-gather.28
  546.4 139.2 all-reduce.8
  755.5 120.4 all-gather.30
  883.6 139.2 all-reduce.10
  1131.4 118.9 all-gather.32
  1256.4 71.2 reduce-scatter.3
  1397.0 119.7 all-gather.34
  1522.8 71.3 reduce-scatter.5
  1663.3 119.7 all-gather.36
  1789.0 71.3 reduce-scatter.7
